TPU v7x, 32 devices: a whole 2x2x4 slice. The times are simulated.
32 devices in a mesh: lat: 8 (over y, x, core), lev: 4 (over z).
Axes of the slice: x: 2, y: 2, z: 4, core: 2. Of those that a mesh axis runs over, the one named last changes fastest.
Arguments:
- grid_adjoint: float32 [2, 96, 640, 1280], P(None, 'lev', 'lat'), may hold values from -6 to 6
- trajectory: bfloat16 [2, 96, 640, 1280], P(None, 'lev', 'lat'), may hold values from -5 to 5
- pair_order: int32 [320], replicated, may hold values from 0 to 319, each once
- legendre: bfloat16 [320, 640, 641], P('lat'), may hold values from -0.25 to 0.25
- modes: bfloat16 [96, 96], replicated, may hold values from -0.625 to 0.625
- rates: float32 [96], replicated, may hold values from 0.5 to 50
Outputs:
- grid_out: float32 [2, 96, 640, 1280], P(None, 'lev', 'lat')
Inputs may be any that keep to these rules, and one draw needn't show every extreme that they name: `pair_order`: A permutation: entry s names the pair k and 639 - k whose basis values are row s of legendre.
All inputs are finite; a program needn't handle non-finite values.
Results may differ from a plain program's by a relative error of at most 0.0068.
Values may be sent and summed in bfloat16 or wider, within the bound.
A program may use at most 192 MiB of HBM per device.

v0:
```python
import math
import jax
import jax.numpy as jnp
from jax import lax
from jax.sharding import PartitionSpec as P


def tables(length, number):
    row = lax.broadcasted_iota(jnp.int32, (length, 2 * number), 0)
    col = lax.broadcasted_iota(jnp.int32, (length, 2 * number), 1)
    wavenum = col % number
    phases = 2.0 * math.pi / length * (row * wavenum % length).astype(jnp.float32)
    forward = (jnp.where(col < number, jnp.cos(phases), -jnp.sin(phases)) / length).astype(
        jnp.bfloat16
    )
    inrow = lax.broadcasted_iota(jnp.int32, (2 * number, length), 0)
    position = lax.broadcasted_iota(jnp.int32, (2 * number, length), 1)
    inwave = inrow % number
    inphase = 2.0 * math.pi / length * (position * inwave % length).astype(jnp.float32)
    weights = jnp.where(inwave == 0, 1.0, 2.0).astype(jnp.float32)
    inverse = jnp.where(
        inrow < number, weights * jnp.cos(inphase), -weights * jnp.sin(inphase)
    ).astype(jnp.bfloat16)
    return (forward, inverse)


def degrees(waves_a, truncation):
    column = lax.broadcasted_iota(jnp.int32, (waves_a.shape[0], truncation + 1), 1)
    lower_part = column < (truncation - waves_a)[:, None]
    degree = jnp.where(lower_part, waves_a[:, None] + column, column - 1)
    degree_ratio = (degree * (degree + 1)).astype(jnp.float32) / float(
        truncation * (truncation + 1)
    )
    return (lower_part, degree_ratio)


def per_device(grid_adjoint, trajectory, pair_order, legendre, modes, rates):
    fields, levels, lat_rows, longitudes = grid_adjoint.shape
    wave_count = longitudes // 2
    slot_count = legendre.shape[0]
    lat_count = legendre.shape[1]
    primary = trajectory[0].astype(jnp.float32)
    coupling = trajectory[1].astype(jnp.float32)
    coupled = jnp.stack(
        [
            primary * grid_adjoint[0] + coupling * grid_adjoint[1],
            coupling * grid_adjoint[0] + primary * grid_adjoint[1],
        ]
    ).astype(jnp.bfloat16)
    forward, inverse = tables(longitudes, wave_count)
    fourier_local = jnp.dot(
        coupled.reshape(-1, longitudes), forward, preferred_element_type=jnp.float32
    )
    fourier_local = fourier_local.astype(jnp.bfloat16).reshape(
        fields, levels, lat_rows, 2, wave_count
    )
    column_order = jnp.stack([pair_order, wave_count - 1 - pair_order], axis=1).reshape(-1)
    permuted = jnp.take(fourier_local, column_order, axis=4)
    received_bands = lax.all_to_all(permuted, "lat", split_axis=4, concat_axis=2, tiled=True)
    grouped = received_bands.reshape(fields, levels, lat_count, 2, slot_count, 2)
    band_index = lax.axis_index("lat")
    local_waves = lax.dynamic_slice_in_dim(pair_order, band_index * slot_count, slot_count)
    lower_part, degree_ratio = degrees(local_waves, wave_count)
    products = jnp.einsum(
        "slj,fvlcsh->sfvchj", legendre, grouped, preferred_element_type=jnp.float32
    )
    lower_mask = lower_part[:, None, None, None, :]
    spectral = jnp.where(lower_mask, products[:, :, :, :, 0], products[:, :, :, :, 1])
    damped = spectral[:, 0] / (1.0 + 4.0 * degree_ratio * degree_ratio)[:, None, None, :]
    rounded = spectral[:, 1].astype(jnp.bfloat16)
    level_index = lax.axis_index("lev")
    lev_count = lax.axis_size("lev")
    flattened = jnp.transpose(rounded, (1, 0, 2, 3)).reshape(levels, -1)
    column_total = flattened.shape[1]
    column_width = -(-column_total // lev_count)
    padding = column_width * lev_count - column_total
    padded = jnp.pad(flattened, ((0, 0), (0, padding)))
    columns = lax.all_to_all(padded, "lev", split_axis=1, concat_axis=0, tiled=True)
    ratio_flat = jnp.broadcast_to(
        degree_ratio[:, None, :], (slot_count, 2, wave_count + 1)
    ).reshape(-1)
    ratio_flat = jnp.pad(ratio_flat, (0, padding))
    ratio_piece = lax.dynamic_slice_in_dim(ratio_flat, level_index * column_width, column_width)
    projected = jnp.einsum("km,kn->mn", modes, columns, preferred_element_type=jnp.float32)
    factor = 1.0 / (1.0 + rates[:, None] * ratio_piece[None, :])
    weighted = (projected * factor).astype(jnp.bfloat16)
    solved_columns = jnp.dot(modes, weighted, preferred_element_type=jnp.float32)
    returned_levels = lax.all_to_all(
        solved_columns.astype(jnp.bfloat16), "lev", split_axis=0, concat_axis=1, tiled=True
    ).astype(solved_columns.dtype)
    solved = returned_levels[:, :column_total].reshape(levels, slot_count, 2, wave_count + 1)
    solved = jnp.transpose(solved, (1, 0, 2, 3))
    updated = jnp.stack([damped, solved], axis=1).astype(jnp.bfloat16)
    zero_value = jnp.zeros((), jnp.bfloat16)
    halves = jnp.stack(
        [jnp.where(lower_mask, updated, zero_value), jnp.where(lower_mask, zero_value, updated)],
        axis=-2,
    )
    synthesised = jnp.einsum(
        "slj,sfvchj->fvlcsh", legendre, halves, preferred_element_type=jnp.float32
    )
    synthesised = synthesised.astype(jnp.bfloat16).reshape(
        fields, levels, lat_count, 2, slot_count * 2
    )
    returned = lax.all_to_all(synthesised, "lat", split_axis=2, concat_axis=4, tiled=True)
    inverse_order = (
        jnp.zeros((wave_count,), jnp.int32)
        .at[column_order]
        .set(jnp.arange(wave_count, dtype=jnp.int32))
    )
    natural = jnp.take(returned, inverse_order, axis=4)
    grid_out = jnp.dot(
        natural.reshape(-1, 2 * wave_count), inverse, preferred_element_type=jnp.float32
    )
    return grid_out.reshape(fields, levels, lat_rows, longitudes)


def solution(mesh):
    placed = (
        P(None, "lev", "lat", None),
        P(None, "lev", "lat", None),
        P(),
        P("lat", None, None),
        P(),
        P(),
    )
    return jax.shard_map(
        per_device,
        mesh=mesh,
        in_specs=placed,
        out_specs=P(None, "lev", "lat", None),
        check_vma=False,
    )
```

profile of v0, /device:TPU:0, one launch (start us, length us, event | category | flops | bytes accessed | tf_op | source)
XLA Modules:
  0.0 961.1 jit_solution(389869084658848675)
XLA Ops:
  0.1 0.7 broadcast_subtract_fusion
  0.7 0.7 stack.30
  1.4 0.1 copy.62
  1.8 14.9 %fusion.9 = (bf16[1,24,80,1280]{3,2,1,0:T(8,128)(2,1)}, bf16[1,24,80,1280]{3,2,1,0:T(8,128)(2,1)}) fusion(f32[2,24,80,1280]{3,2,1,0:T(8,128)} %param.8, bf16[2,24,80,1280]{3,2,1,0:T(8,128)(2,1)} %param.9), kind=kLoop, calls=%fused_computation.25 | loop fusion | flops 24576000 | bytes 39321600 | tf_op jit(solution)/shard_map/convert.8
  16.6 8.6 pad_maximum_fusion.1
  25.3 27.6 %multiply_convert_fusion.4 = bf16[1280,1280]{1,0:T(8,128)(2,1)S(1)} fusion(s32[1280]{0:T(1024)S(1)} %get-tuple-element.14, s32[1280]{0:T(1024)S(1)} %get-tuple-element.15, pred[1280]{0:T(1024)(128)(4,1)S(1)} %get-tuple-element.17, pred[1280]{0:T(1024)(128)(4,1)S(1)} %get-tuple-element.16), kind=kLoop, calls=%fused_computation.47.clone.clone.1 | loop fusion | flops 22937600 | bytes 3289600 | tf_op jit(solution)/shard_map/dot_general | solution.py:51
  52.9 19.0 %convolution_convert_fusion.1 = bf16[3840,1280]{1,0:T(8,128)(2,1)} fusion(bf16[3840,1280]{1,0:T(8,128)(2,1)} %bitcast.82, bf16[1280,1280]{1,0:T(8,128)(2,1)S(1)} %multiply_convert_fusion.4), kind=kOutput, calls=%fused_computation.14 | convolution fusion | flops 12587827200 | bytes 22937600 | tf_op jit(solution)/shard_map/dot_general | solution.py:51
  71.9 19.3 %reshape.233 = bf16[2,24,80,2,640]{4,3,2,1,0:T(2,128)(2,1)} reshape(bf16[3840,1280]{1,0:T(8,128)(2,1)} %convolution_convert_fusion.1) | data formatting | bytes 19660800 | tf_op jit(solution)/shard_map/reshape | solution.py:54
  91.2 25.9 %copy.64 = bf16[2,24,80,2,640]{2,1,3,0,4:T(8,128)(2,1)} copy(bf16[2,24,80,2,640]{4,3,2,1,0:T(2,128)(2,1)} %reshape.233) | data formatting | bytes 19660800 | tf_op jit(solution)/shard_map/reshape | solution.py:54
  117.1 25.2 %gather_fusion = bf16[640,2,24,80,2]{3,2,4,1,0:T(8,128)(2,1)} fusion(bf16[2,24,80,2,640]{2,1,3,0,4:T(8,128)(2,1)} %copy.64, s32[1024]{0:T(1024)S(1)} %pad_clamp_fusion.1), kind=kCustom, calls=%fused_computation.clone | custom fusion | bytes 19663360 | tf_op jit(solution)/shard_map/jit(_take)/gather | solution.py:58
  142.3 14.0 %select_bitcast_fusion.1 = bf16[2,24,80,2,640]{2,1,3,0,4:T(8,128)(2,1)} fusion(bf16[640,2,24,80,2]{3,2,4,1,0:T(8,128)(2,1)} %gather_fusion, pred[640]{0:T(1024)(128)(4,1)S(1)} %compare_and_fusion.1), kind=kLoop, calls=%fused_computation.9 | loop fusion | flops 4915200 | bytes 19661440 | tf_op jit(solution)/shard_map/jit(_take)/select_n | solution.py:58
  156.3 5.6 all-to-all-start
  162.0 0.8 broadcast_subtract_fusion.1
  162.8 172.5 %all-to-all-done = bf16[2,24,80,2,640]{2,1,3,0,4:T(8,128)(2,1)} async-done(((bf16[2,24,80,2,640]{2,1,3,0,4:T(8,128)(2,1)}), bf16[2,24,80,2,640]{2,1,3,0,4:T(8,128)(2,1)}, u32[]{:S(2)}, u32[]{:S(2)}) %all-to-all-start) | async-done | bytes 9830432 | tf_op jit(solution)/shard_map/all_to_all | solution.py:59
  335.4 27.2 %copy.104 = bf16[2,24,80,2,8,80]{2,4,1,5,3,0:T(8,128)(2,1)} copy(bf16[2,24,80,2,8,80]{2,1,3,0,5,4:T(8,128)(2,1)} %bitcast.2) | data formatting | bytes 19660800 | tf_op jit(solution)/shard_map/all_to_all | solution.py:59
  362.6 23.1 %reshape.235 = bf16[2,24,640,2,40,2]{2,1,5,4,3,0:T(8,128)(2,1)} reshape(bf16[2,24,8,80,2,80]{3,2,1,5,4,0:T(8,128)(2,1)} %bitcast.76) | data formatting | bytes 19660800 | tf_op jit(solution)/shard_map/reshape | solution.py:60
  385.6 29.7 %fusion.2 = f32[40,2,24,2,2,641]{5,2,4,3,1,0:T(8,128)} fusion(bf16[40,640,641,1,1,1]{1,0,2,5,4,3:T(8,128)(2,1)} %bitcast.79, bf16[2,24,640,2,40,2]{2,1,5,4,3,0:T(8,128)(2,1)} %reshape.235), kind=kOutput, calls=%fused_computation.5 | convolution fusion | flops 6301286400 | bytes 62341120 | tf_op jit(solution)/shard_map/slj,fvlcsh->sfvchj/dot_general | solution.py:64
  415.3 9.1 fusion.6
  424.5 4.5 copy-done.2
  429.0 0.4 fusion.52
  429.4 2.3 copy.69
  431.7 3.7 all_to_all.51
  435.4 3.4 copy.70
  438.8 15.4 %all-to-all-start.1 = ((bf16[24,4,12820]{2,0,1:T(8,128)(2,1)}), bf16[24,4,12820]{2,0,1:T(8,128)(2,1)S(1)}, u32[]{:S(2)}, u32[]{:S(2)}) async-start(bf16[24,4,12820]{2,0,1:T(8,128)(2,1)} %copy.70), calls=%async_computation.1 | async-start | bytes 4964352 | tf_op jit(solution)/shard_map/all_to_all | solution.py:78
  454.4 0.3 reshape.236
  454.8 52.9 %all-to-all-done.1 = bf16[24,4,12820]{2,0,1:T(8,128)(2,1)S(1)} async-done(((bf16[24,4,12820]{2,0,1:T(8,128)(2,1)}), bf16[24,4,12820]{2,0,1:T(8,128)(2,1)S(1)}, u32[]{:S(2)}, u32[]{:S(2)}) %all-to-all-start.1) | async-done | bytes 2461472 | tf_op jit(solution)/shard_map/all_to_all | solution.py:78
  507.7 3.0 convolution_convert_fusion
  510.7 4.5 all-to-all-start.2
  515.3 3.4 fusion.53
  518.7 52.7 %all-to-all-done.2 = bf16[4,24,12820]{2,1,0:T(8,128)(2,1)} async-done(((bf16[4,24,12820]{2,1,0:T(8,128)(2,1)}), bf16[4,24,12820]{2,1,0:T(8,128)(2,1)}, u32[]{:S(2)}, u32[]{:S(2)}) %all-to-all-start.2) | async-done | bytes 2461472 | tf_op jit(solution)/shard_map/all_to_all | solution.py:88
  571.3 4.1 copy.71
  575.5 10.8 %convert_element_type.92 = bf16[24,40,2,641]{3,2,1,0:T(2,128)(2,1)} reshape(bf16[24,4,12820]{2,1,0:T(4,128)(2,1)} %copy.71) | data formatting | bytes 4922880 | tf_op jit(solution)/shard_map/convert_element_type | solution.py:90
  586.3 2.8 copy.105
  589.1 2.2 broadcast_select_fusion.1
  591.3 22.3 %convert_bitcast_fusion = bf16[2,24,640,2,40,2]{2,1,5,3,0,4:T(8,128)(2,1)} fusion(bf16[40,640,641,1,1,1]{1,0,2,5,4,3:T(8,128)(2,1)} %bitcast.80, bf16[40,2,24,2,1,641]{5,2,3,0,4,1:T(8,128)(2,1)S(1)} %get-tuple-element.11, bf16[40,2,24,2,1,641]{5,2,3,0,4,1:T(8,128)(2,1)S(1)} %get-tuple-element.10), kind=kOutput, calls=%fused_computation.31 | convolution fusion | flops 6311124480 | bytes 52495360 | tf_op jit(solution)/shard_map/slj,sfvchj->fvlcsh/dot_general | solution.py:99
  613.6 8.4 copy.75
  622.0 20.1 %copy.76 = bf16[2,24,640,2,80]{4,1,3,0,2:T(8,128)(2,1)} copy(bf16[2,24,640,2,80]{2,1,4,3,0:T(8,128)(2,1)} %bitcast.78) | data formatting | bytes 19660800 | tf_op jit(solution)/shard_map/reshape | solution.py:102
  642.2 6.0 all-to-all-start.3
  648.2 0.1 reshape.238
  648.3 4.1 scatter_custom_fusion
  652.5 30.0 %fusion.83 = bf16[1280,1280,1,1]{1,0,3,2:T(8,128)(2,1)S(1)} fusion(s32[1280]{0:T(1024)S(1)} %copy-done.6, s32[1280]{0:T(1024)S(1)} %copy-done.8, pred[1280]{0:T(1024)(128)(4,1)S(1)} %copy-done.12, pred[1280]{0:T(1024)(128)(4,1)S(1)} %copy-done.10), kind=kLoop, calls=%fused_computation.59.clone.clone.1 | loop fusion | flops 27852800 | bytes 3289600 | tf_op jit(solution)/shard_map/dot_general | solution.py:112
  682.5 138.4 %all-to-all-done.3 = bf16[2,24,640,2,80]{4,1,3,0,2:T(8,128)(2,1)} async-done(((bf16[2,24,640,2,80]{4,1,3,0,2:T(8,128)(2,1)}), bf16[2,24,640,2,80]{4,1,3,0,2:T(8,128)(2,1)}, u32[]{:S(2)}, u32[]{:S(2)}) %all-to-all-start.3) | async-done | bytes 9830432 | tf_op jit(solution)/shard_map/all_to_all | solution.py:105
  820.9 33.7 %copy.87 = bf16[2,24,80,2,8,80]{2,1,3,0,5,4:T(8,128)(2,1)} copy(bf16[2,24,80,2,8,80]{5,1,3,0,2,4:T(8,128)(2,1)} %bitcast.31) | data formatting | bytes 19660800 | tf_op jit(solution)/shard_map/all_to_all | solution.py:105
  854.6 25.0 %gather_fusion.1 = bf16[640,2,24,80,2]{3,2,4,1,0:T(8,128)(2,1)} fusion(bf16[2,24,80,2,640]{2,1,3,0,4:T(8,128)(2,1)} %bitcast.77, s32[1024]{0:T(1024)S(1)} %pad_clamp_fusion), kind=kCustom, calls=%fused_computation.1.clone | custom fusion | bytes 19663360 | tf_op jit(solution)/shard_map/jit(_take)/gather | solution.py:111
  879.5 14.0 %select_bitcast_fusion = bf16[2,24,80,2,640]{2,1,3,0,4:T(8,128)(2,1)} fusion(bf16[640,2,24,80,2]{3,2,4,1,0:T(8,128)(2,1)} %gather_fusion.1, pred[640]{0:T(1024)(128)(4,1)S(1)} %compare_and_fusion), kind=kLoop, calls=%fused_computation.8 | loop fusion | flops 4915200 | bytes 19661440 | tf_op jit(solution)/shard_map/jit(_take)/select_n | solution.py:111
  893.6 26.9 %copy.79 = bf16[2,24,80,2,640]{4,3,2,1,0:T(2,128)(2,1)} copy(bf16[2,24,80,2,640]{2,1,3,0,4:T(8,128)(2,1)} %select_bitcast_fusion) | data formatting | bytes 19660800 | tf_op jit(solution)/shard_map/jit(_take)/select_n | solution.py:111
  920.5 21.8 %dot_general.28 = bf16[2,24,80,1280]{3,2,1,0:T(8,128)(2,1)} reshape(bf16[2,24,80,2,640]{4,3,2,1,0:T(2,128)(2,1)} %copy.79) | data formatting | bytes 19660800 | tf_op jit(solution)/shard_map/dot_general | solution.py:112
  942.3 18.3 %fusion.33 = f32[2,24,80,1280]{3,2,1,0:T(8,128)} fusion(bf16[2,24,80,1280]{3,2,1,0:T(8,128)(2,1)} %dot_general.28, bf16[1280,1280,1,1]{1,0,3,2:T(8,128)(2,1)S(1)} %fusion.83), kind=kOutput, calls=%fused_computation.60 | convolution fusion | flops 12582912000 | bytes 32768000 | tf_op jit(solution)/shard_map/dot_general | solution.py:112
  (45 shorter events, 0.7 us)
Async XLA Ops:
  0.0 507.7 %copy-start = (bf16[96,96]{1,0:T(8,128)(2,1)S(1)}, bf16[96,96]{1,0:T(8,128)(2,1)}, u32[]{:S(2)}) copy-start(bf16[96,96]{1,0:T(8,128)(2,1)} %param.12) | copy-start | bytes 55300
  0.0 25.3 %copy-start.5 = (s32[1280]{0:T(1024)}, s32[1280]{0:T(1024)S(1)}, u32[]{:S(2)}) copy-start(s32[1280]{0:T(1024)S(1)} %get-tuple-element.14) | copy-start | bytes 15364
  0.0 25.3 %copy-start.7 = (s32[1280]{0:T(1024)}, s32[1280]{0:T(1024)S(1)}, u32[]{:S(2)}) copy-start(s32[1280]{0:T(1024)S(1)} %get-tuple-element.15) | copy-start | bytes 15364
  0.0 25.2 %copy-start.9 = (pred[1280]{0:T(1024)(128)(4,1)}, pred[1280]{0:T(1024)(128)(4,1)S(1)}, u32[]{:S(2)}) copy-start(pred[1280]{0:T(1024)(128)(4,1)S(1)} %get-tuple-element.16) | copy-start | bytes 3844
  0.1 25.2 %copy-start.11 = (pred[1280]{0:T(1024)(128)(4,1)}, pred[1280]{0:T(1024)(128)(4,1)S(1)}, u32[]{:S(2)}) copy-start(pred[1280]{0:T(1024)(128)(4,1)S(1)} %get-tuple-element.17) | copy-start | bytes 3844
  1.6 15.0 %copy-start.3 = (s32[320,2]{1,0:T(8,128)}, s32[320,2]{1,0:T(8,128)S(1)}, u32[]{:S(2)}) copy-start(s32[320,2]{1,0:T(8,128)S(1)} %copy.62) | copy-start | bytes 7684
  156.3 179.0 %all-to-all-start = ((bf16[2,24,80,2,640]{2,1,3,0,4:T(8,128)(2,1)}), bf16[2,24,80,2,640]{2,1,3,0,4:T(8,128)(2,1)}, u32[]{:S(2)}, u32[]{:S(2)}) async-start(bf16[2,24,80,2,640]{2,1,3,0,4:T(8,128)(2,1)} %select_bitcast_fusion.1), calls=%async_computation | async-start | bytes 31457280 | tf_op jit(solution)/shard_map/all_to_all | solution.py:59
  424.5 4.5 copy-start.2
  435.4 72.3 %copy-start.13 = (f32[96]{0:T(128)S(1)}, f32[96]{0:T(128)}, u32[]{:S(2)}) copy-start(f32[96]{0:T(128)} %param.13) | copy-start | bytes 1156
  438.8 68.9 %all-to-all-start.1 = ((bf16[24,4,12820]{2,0,1:T(8,128)(2,1)}), bf16[24,4,12820]{2,0,1:T(8,128)(2,1)S(1)}, u32[]{:S(2)}, u32[]{:S(2)}) async-start(bf16[24,4,12820]{2,0,1:T(8,128)(2,1)} %copy.70), calls=%async_computation.1 | async-start | bytes 4964352 | tf_op jit(solution)/shard_map/all_to_all | solution.py:78
  510.7 60.6 %all-to-all-start.2 = ((bf16[4,24,12820]{2,1,0:T(8,128)(2,1)}), bf16[4,24,12820]{2,1,0:T(8,128)(2,1)}, u32[]{:S(2)}, u32[]{:S(2)}) async-start(bf16[4,24,12820]{2,1,0:T(8,128)(2,1)} %bitcast.84), calls=%async_computation.2 | async-start | bytes 4964352 | tf_op jit(solution)/shard_map/all_to_all | solution.py:88
  642.1 6.0 copy-start.4
  642.1 10.4 %copy-start.6 = (s32[1280]{0:T(1024)S(1)}, s32[1280]{0:T(1024)}, u32[]{:S(2)}) copy-start(s32[1280]{0:T(1024)} %copy-done.5) | copy-start | bytes 15364
  642.1 10.4 %copy-start.8 = (s32[1280]{0:T(1024)S(1)}, s32[1280]{0:T(1024)}, u32[]{:S(2)}) copy-start(s32[1280]{0:T(1024)} %copy-done.7) | copy-start | bytes 15364
  642.1 10.4 %copy-start.10 = (pred[1280]{0:T(1024)(128)(4,1)S(1)}, pred[1280]{0:T(1024)(128)(4,1)}, u32[]{:S(2)}) copy-start(pred[1280]{0:T(1024)(128)(4,1)} %copy-done.9) | copy-start | bytes 3844
  642.1 10.4 %copy-start.12 = (pred[1280]{0:T(1024)(128)(4,1)S(1)}, pred[1280]{0:T(1024)(128)(4,1)}, u32[]{:S(2)}) copy-start(pred[1280]{0:T(1024)(128)(4,1)} %copy-done.11) | copy-start | bytes 3844
  642.2 178.7 %all-to-all-start.3 = ((bf16[2,24,640,2,80]{4,1,3,0,2:T(8,128)(2,1)}), bf16[2,24,640,2,80]{4,1,3,0,2:T(8,128)(2,1)}, u32[]{:S(2)}, u32[]{:S(2)}) async-start(bf16[2,24,640,2,80]{4,1,3,0,2:T(8,128)(2,1)} %copy.76), calls=%async_computation.3 | async-start | bytes 31457280 | tf_op jit(solution)/shard_map/all_to_all | solution.py:105
  942.3 18.3 %copy-start.1 = (bf16[96,96]{1,0:T(8,128)(2,1)S(1)}, bf16[96,96]{1,0:T(8,128)(2,1)}, u32[]{:S(2)}) copy-start(bf16[96,96]{1,0:T(8,128)(2,1)} %param.12) | copy-start | bytes 55300
where the time goes:
time: 973 us; the launch traced here: 961 us
  waiting for transfers between devices  416 us (43%)
  local copies, waits for them, and re-layouts  294 us (30%)
  other arithmetic  125 us (13%)
  matrix products  92.3 us (9%)
  starting transfers between devices  31.6 us (3%)
    all_to_all x1, waiting for transfers between devices, per_device(): lax.all_to_all(permuted, 'lat', split_axis=4, concat_axis=2, tiled=True)  173 us
    all_to_all x1, waiting for transfers between devices, per_device(): lax.all_to_all(synthesised, 'lat', split_axis=2, concat_axis=4, tiled=True)  138 us
    all_to_all x1, waiting for transfers between devices, per_device(): lax.all_to_all(padded, 'lev', split_axis=1, concat_axis=0, tiled=True)  52.9 us
    all_to_all x1, waiting for transfers between devices, per_device(): lax.all_to_all(solved_columns.astype(jnp.bfloat16), 'lev', split_axis=0,...  52.7 us
    reshape x2, local copies, waits for them, and re-layouts, per_device(): fourier_local.astype(jnp.bfloat16)  45.2 us
    all_to_all x1, local copies, waits for them, and re-layouts, per_device(): lax.all_to_all(synthesised, 'lat', split_axis=2, concat_axis=4, tiled=True)  33.7 us
    dot_general x1, other arithmetic, per_device(): jnp.dot(natural.reshape(-1, 2 * wave_count), inverse, preferred_element_t...  30 us
    dot_general x1, matrix products, per_device(): jnp.einsum('slj,fvlcsh->sfvchj', legendre, grouped, preferred_element_typ...  29.7 us
  transfers between devices with their start and end apart: 4, of which 4 were waited for; matrix products, arithmetic and copies ran while one was open for 4% of the time, Pallas kernels for 0%

commit v1 on v0

--- a/solution.py
+++ b/solution.py
@@ -56,7 +56,10 @@
     )
     column_order = jnp.stack([pair_order, wave_count - 1 - pair_order], axis=1).reshape(-1)
     permuted = jnp.take(fourier_local, column_order, axis=4)
-    received_bands = lax.all_to_all(permuted, "lat", split_axis=4, concat_axis=2, tiled=True)
+    received_bands = jnp.concatenate(
+        lax.all_to_all(jnp.stack(jnp.split(permuted, lax.axis_size("lat"), axis=4)), "lat", 0, 0),
+        axis=2,
+    )
     grouped = received_bands.reshape(fields, levels, lat_count, 2, slot_count, 2)
     band_index = lax.axis_index("lat")
     local_waves = lax.dynamic_slice_in_dim(pair_order, band_index * slot_count, slot_count)

time: 973 us -> 977 us (level)
  local copies, waits for them, and re-layouts: 294 us -> 307 us
    all_to_all x1 -> x0, local copies, waits for them, and re-layouts: 27.2 us -> none  [per_device(): lax.all_to_all(permuted, 'lat', split_axis=4, concat_axis=2, tiled=True)]
    another operation x0 -> x2, local copies, waits for them, and re-layouts: none -> 24.7 us  [the longest x1 23.1 us: per_device(): received_bands.reshape(fields, levels, lat_count, 2, slot_count, 2)]
    unnamed x28 -> x33, local copies, waits for them, and re-layouts: 4.56 us -> 15.8 us
where the time goes in v1:
time: 977 us; the launch traced here: 964 us
  waiting for transfers between devices  421 us (43%)
  local copies, waits for them, and re-layouts  307 us (31%)
  other arithmetic  121 us (12%)
  matrix products  92.3 us (9%)
  starting transfers between devices  22.4 us (2%)
    all_to_all x1, waiting for transfers between devices, per_device(): lax.all_to_all(jnp.stack(jnp.split(permuted, lax.axis_size('lat'), axis=4...  173 us
    all_to_all x1, waiting for transfers between devices, per_device(): lax.all_to_all(synthesised, 'lat', split_axis=2, concat_axis=4, tiled=True)  143 us
    all_to_all x1, waiting for transfers between devices, per_device(): lax.all_to_all(padded, 'lev', split_axis=1, concat_axis=0, tiled=True)  52.9 us
    all_to_all x1, waiting for transfers between devices, per_device(): lax.all_to_all(solved_columns.astype(jnp.bfloat16), 'lev', split_axis=0,...  52.7 us
    reshape x2, local copies, waits for them, and re-layouts, per_device(): fourier_local.astype(jnp.bfloat16)  45.2 us
    all_to_all x1, local copies, waits for them, and re-layouts, per_device(): lax.all_to_all(synthesised, 'lat', split_axis=2, concat_axis=4, tiled=True)  33.7 us
    dot_general x1, other arithmetic, per_device(): jnp.dot(natural.reshape(-1, 2 * wave_count), inverse, preferred_element_t...  30 us
    dot_general x1, matrix products, per_device(): jnp.einsum('slj,fvlcsh->sfvchj', legendre, grouped, preferred_element_typ...  29.7 us
  transfers between devices with their start and end apart: 4, of which 4 were waited for; matrix products, arithmetic and copies ran while one was open for 4% of the time, Pallas kernels for 0%

profile of v1, /device:TPU:0, one launch (start us, length us, event | category | flops | bytes accessed | tf_op | source)
XLA Modules:
  0.0 964.4 jit_solution(2943579033215104258)
XLA Ops:
  1.9 14.9 %fusion.9 = (bf16[1,24,80,1280]{3,2,1,0:T(8,128)(2,1)}, bf16[1,24,80,1280]{3,2,1,0:T(8,128)(2,1)}) fusion(f32[2,24,80,1280]{3,2,1,0:T(8,128)} %param.8, bf16[2,24,80,1280]{3,2,1,0:T(8,128)(2,1)} %param.9), kind=kLoop, calls=%fused_computation.24 | loop fusion | flops 24576000 | bytes 39321600 | tf_op jit(solution)/shard_map/convert.8
  16.8 8.6 pad_maximum_fusion.1
  25.4 27.6 %multiply_convert_fusion.4 = bf16[1280,1280]{1,0:T(8,128)(2,1)S(1)} fusion(s32[1280]{0:T(1024)S(1)} %get-tuple-element.14, s32[1280]{0:T(1024)S(1)} %get-tuple-element.15, pred[1280]{0:T(1024)(128)(4,1)S(1)} %get-tuple-element.17, pred[1280]{0:T(1024)(128)(4,1)S(1)} %get-tuple-element.16), kind=kLoop, calls=%fused_computation.46.clone.clone.1 | loop fusion | flops 22937600 | bytes 3289600 | tf_op jit(solution)/shard_map/dot_general | solution.py:51
  53.0 19.0 %convolution_convert_fusion.1 = bf16[3840,1280]{1,0:T(8,128)(2,1)} fusion(bf16[3840,1280]{1,0:T(8,128)(2,1)} %bitcast.110, bf16[1280,1280]{1,0:T(8,128)(2,1)S(1)} %multiply_convert_fusion.4), kind=kOutput, calls=%fused_computation.13 | convolution fusion | flops 12587827200 | bytes 22937600 | tf_op jit(solution)/shard_map/dot_general | solution.py:51
  72.0 19.3 %reshape.232 = bf16[2,24,80,2,640]{4,3,2,1,0:T(2,128)(2,1)} reshape(bf16[3840,1280]{1,0:T(8,128)(2,1)} %convolution_convert_fusion.1) | data formatting | bytes 19660800 | tf_op jit(solution)/shard_map/reshape | solution.py:54
  91.3 25.9 %copy.64 = bf16[2,24,80,2,640]{2,1,3,0,4:T(8,128)(2,1)} copy(bf16[2,24,80,2,640]{4,3,2,1,0:T(2,128)(2,1)} %reshape.232) | data formatting | bytes 19660800 | tf_op jit(solution)/shard_map/reshape | solution.py:54
  117.2 4.3 scatter_custom_fusion
  122.2 25.0 %gather_fusion = bf16[640,2,24,80,2]{3,2,4,1,0:T(8,128)(2,1)} fusion(bf16[2,24,80,2,640]{2,1,3,0,4:T(8,128)(2,1)} %copy.64, s32[1024]{0:T(1024)S(1)} %get-tuple-element.19), kind=kCustom, calls=%fused_computation.clone | custom fusion | bytes 19663360 | tf_op jit(solution)/shard_map/jit(_take)/gather | solution.py:58
  147.1 8.8 select_bitcast_fusion.1
  155.9 1.6 fusion.61
  157.5 1.6 fusion.60
  159.1 1.6 fusion.59
  160.8 1.6 fusion.58
  162.4 1.6 fusion.57
  164.0 1.6 fusion.56
  165.6 1.6 fusion.55
  168.8 6.1 all-to-all-start
  175.7 172.5 %all-to-all-done = bf16[8,2,24,80,2,80]{3,2,4,1,5,0:T(8,128)(2,1)} async-done(((bf16[8,2,24,80,2,80]{3,2,4,1,5,0:T(8,128)(2,1)}), bf16[8,2,24,80,2,80]{3,2,4,1,5,0:T(8,128)(2,1)}, u32[]{:S(2)}, u32[]{:S(2)}) %all-to-all-start) | async-done | bytes 9830432 | tf_op jit(solution)/shard_map/all_to_all | solution.py:60
  348.3 27.2 %copy.65 = bf16[2,24,8,80,2,80]{3,2,1,5,4,0:T(8,128)(2,1)} copy(bf16[2,24,8,80,2,80]{3,1,4,0,5,2:T(8,128)(2,1)} %bitcast.10) | data formatting | bytes 19660800 | tf_op jit(solution)/shard_map/reshape | solution.py:59
  375.5 23.1 %reshape_reshape.3 = bf16[2,24,640,2,40,2]{2,1,5,4,3,0:T(8,128)(2,1)} reshape(bf16[2,24,8,80,2,80]{3,2,1,5,4,0:T(8,128)(2,1)} %copy.65) | data formatting | bytes 19660800 | tf_op jit(solution)/shard_map/reshape;reshape | solution.py:63
  398.5 29.7 %fusion.2 = f32[40,2,24,2,2,641]{5,2,4,3,1,0:T(8,128)} fusion(bf16[40,640,641,1,1,1]{1,0,2,5,4,3:T(8,128)(2,1)} %bitcast.107, bf16[2,24,640,2,40,2]{2,1,5,4,3,0:T(8,128)(2,1)} %reshape_reshape.3), kind=kOutput, calls=%fused_computation.5 | convolution fusion | flops 6301286400 | bytes 62341120 | tf_op jit(solution)/shard_map/slj,fvlcsh->sfvchj/dot_general | solution.py:67
  428.2 9.1 fusion.6
  437.4 4.5 copy-done.2
  442.3 2.3 copy.69
  444.6 3.7 all_to_all.41
  448.3 3.4 copy.70
  451.7 5.8 all-to-all-start.1
  458.2 52.9 %all-to-all-done.1 = bf16[24,4,12820]{2,0,1:T(8,128)(2,1)S(1)} async-done(((bf16[24,4,12820]{2,0,1:T(8,128)(2,1)}), bf16[24,4,12820]{2,0,1:T(8,128)(2,1)S(1)}, u32[]{:S(2)}, u32[]{:S(2)}) %all-to-all-start.1) | async-done | bytes 2461472 | tf_op jit(solution)/shard_map/all_to_all | solution.py:81
  511.1 3.0 convolution_convert_fusion
  514.1 4.5 all-to-all-start.2
  518.6 3.4 fusion.53
  522.0 52.7 %all-to-all-done.2 = bf16[4,24,12820]{2,1,0:T(8,128)(2,1)} async-done(((bf16[4,24,12820]{2,1,0:T(8,128)(2,1)}), bf16[4,24,12820]{2,1,0:T(8,128)(2,1)}, u32[]{:S(2)}, u32[]{:S(2)}) %all-to-all-start.2) | async-done | bytes 2461472 | tf_op jit(solution)/shard_map/all_to_all | solution.py:91
  574.7 4.1 copy.71
  578.8 10.8 %convert_element_type.92 = bf16[24,40,2,641]{3,2,1,0:T(2,128)(2,1)} reshape(bf16[24,4,12820]{2,1,0:T(4,128)(2,1)} %copy.71) | data formatting | bytes 4922880 | tf_op jit(solution)/shard_map/convert_element_type | solution.py:93
  589.6 2.8 copy.103
  592.4 2.2 broadcast_select_fusion.1
  594.6 22.3 %convert_bitcast_fusion = bf16[2,24,640,2,40,2]{2,1,5,3,0,4:T(8,128)(2,1)} fusion(bf16[40,640,641,1,1,1]{1,0,2,5,4,3:T(8,128)(2,1)} %bitcast.108, bf16[40,2,24,2,1,641]{5,2,3,0,4,1:T(8,128)(2,1)S(1)} %get-tuple-element.11, bf16[40,2,24,2,1,641]{5,2,3,0,4,1:T(8,128)(2,1)S(1)} %get-tuple-element.10), kind=kOutput, calls=%fused_computation.30 | convolution fusion | flops 6311124480 | bytes 52495360 | tf_op jit(solution)/shard_map/slj,sfvchj->fvlcsh/dot_general | solution.py:102
  617.0 8.4 copy.75
  625.4 20.1 %copy.76 = bf16[2,24,640,2,80]{4,1,3,0,2:T(8,128)(2,1)} copy(bf16[2,24,640,2,80]{2,1,4,3,0:T(8,128)(2,1)} %bitcast.106) | data formatting | bytes 19660800 | tf_op jit(solution)/shard_map/reshape | solution.py:105
  645.5 6.0 all-to-all-start.3
  651.5 30.0 %fusion.91 = bf16[1280,1280,1,1]{1,0,3,2:T(8,128)(2,1)S(1)} fusion(s32[1280]{0:T(1024)S(1)} %copy-done.5, s32[1280]{0:T(1024)S(1)} %copy-done.7, pred[1280]{0:T(1024)(128)(4,1)S(1)} %copy-done.11, pred[1280]{0:T(1024)(128)(4,1)S(1)} %copy-done.9), kind=kLoop, calls=%fused_computation.58.clone.clone.1 | loop fusion | flops 27852800 | bytes 3289600 | tf_op jit(solution)/shard_map/dot_general | solution.py:115
  681.5 142.7 %all-to-all-done.3 = bf16[2,24,640,2,80]{4,1,3,0,2:T(8,128)(2,1)} async-done(((bf16[2,24,640,2,80]{4,1,3,0,2:T(8,128)(2,1)}), bf16[2,24,640,2,80]{4,1,3,0,2:T(8,128)(2,1)}, u32[]{:S(2)}, u32[]{:S(2)}) %all-to-all-start.3) | async-done | bytes 9830432 | tf_op jit(solution)/shard_map/all_to_all | solution.py:108
  824.2 33.7 %copy.87 = bf16[2,24,80,2,8,80]{2,1,3,0,5,4:T(8,128)(2,1)} copy(bf16[2,24,80,2,8,80]{5,1,3,0,2,4:T(8,128)(2,1)} %bitcast.38) | data formatting | bytes 19660800 | tf_op jit(solution)/shard_map/all_to_all | solution.py:108
  857.9 25.0 %gather_fusion.1 = bf16[640,2,24,80,2]{3,2,4,1,0:T(8,128)(2,1)} fusion(bf16[2,24,80,2,640]{2,1,3,0,4:T(8,128)(2,1)} %bitcast.105, s32[1024]{0:T(1024)S(1)} %copy-done.3), kind=kCustom, calls=%fused_computation.1.clone | custom fusion | bytes 19663360 | tf_op jit(solution)/shard_map/jit(_take)/gather | solution.py:114
  882.9 14.0 %select_bitcast_fusion = bf16[2,24,80,2,640]{2,1,3,0,4:T(8,128)(2,1)} fusion(bf16[640,2,24,80,2]{3,2,4,1,0:T(8,128)(2,1)} %gather_fusion.1, pred[640]{0:T(1024)(128)(4,1)S(1)} %compare_and_fusion), kind=kLoop, calls=%fused_computation.7 | loop fusion | flops 4915200 | bytes 19661440 | tf_op jit(solution)/shard_map/jit(_take)/select_n | solution.py:114
  896.9 26.9 %copy.79 = bf16[2,24,80,2,640]{4,3,2,1,0:T(2,128)(2,1)} copy(bf16[2,24,80,2,640]{2,1,3,0,4:T(8,128)(2,1)} %select_bitcast_fusion) | data formatting | bytes 19660800 | tf_op jit(solution)/shard_map/jit(_take)/select_n | solution.py:114
  923.8 21.8 %dot_general.28 = bf16[2,24,80,1280]{3,2,1,0:T(8,128)(2,1)} reshape(bf16[2,24,80,2,640]{4,3,2,1,0:T(2,128)(2,1)} %copy.79) | data formatting | bytes 19660800 | tf_op jit(solution)/shard_map/dot_general | solution.py:115
  945.7 18.3 %fusion.33 = f32[2,24,80,1280]{3,2,1,0:T(8,128)} fusion(bf16[2,24,80,1280]{3,2,1,0:T(8,128)(2,1)} %dot_general.28, bf16[1280,1280,1,1]{1,0,3,2:T(8,128)(2,1)S(1)} %fusion.91), kind=kOutput, calls=%fused_computation.59 | convolution fusion | flops 12582912000 | bytes 32768000 | tf_op jit(solution)/shard_map/dot_general | solution.py:115
  (50 shorter events, 5.9 us)
Async XLA Ops:
  0.0 511.1 %copy-start = (bf16[96,96]{1,0:T(8,128)(2,1)S(1)}, bf16[96,96]{1,0:T(8,128)(2,1)}, u32[]{:S(2)}) copy-start(bf16[96,96]{1,0:T(8,128)(2,1)} %param.12) | copy-start | bytes 55300
  0.0 25.4 %copy-start.4 = (s32[1280]{0:T(1024)}, s32[1280]{0:T(1024)S(1)}, u32[]{:S(2)}) copy-start(s32[1280]{0:T(1024)S(1)} %get-tuple-element.14) | copy-start | bytes 15364
  0.0 25.4 %copy-start.6 = (s32[1280]{0:T(1024)}, s32[1280]{0:T(1024)S(1)}, u32[]{:S(2)}) copy-start(s32[1280]{0:T(1024)S(1)} %get-tuple-element.15) | copy-start | bytes 15364
  0.0 25.4 %copy-start.8 = (pred[1280]{0:T(1024)(128)(4,1)}, pred[1280]{0:T(1024)(128)(4,1)S(1)}, u32[]{:S(2)}) copy-start(pred[1280]{0:T(1024)(128)(4,1)S(1)} %get-tuple-element.16) | copy-start | bytes 3844
  0.1 25.4 %copy-start.10 = (pred[1280]{0:T(1024)(128)(4,1)}, pred[1280]{0:T(1024)(128)(4,1)S(1)}, u32[]{:S(2)}) copy-start(pred[1280]{0:T(1024)(128)(4,1)S(1)} %get-tuple-element.17) | copy-start | bytes 3844
  168.8 179.5 %all-to-all-start = ((bf16[8,2,24,80,2,80]{3,2,4,1,5,0:T(8,128)(2,1)}), bf16[8,2,24,80,2,80]{3,2,4,1,5,0:T(8,128)(2,1)}, u32[]{:S(2)}, u32[]{:S(2)}) async-start(bf16[8,2,24,80,2,80]{3,2,4,1,5,0:T(8,128)(2,1)} %fusion.54), calls=%async_computation | async-start | bytes 31457280 | tf_op jit(solution)/shard_map/all_to_all | solution.py:60
  437.4 4.5 copy-start.2
  448.3 62.8 %copy-start.12 = (f32[96]{0:T(128)S(1)}, f32[96]{0:T(128)}, u32[]{:S(2)}) copy-start(f32[96]{0:T(128)} %param.13) | copy-start | bytes 1156
  451.7 59.3 %all-to-all-start.1 = ((bf16[24,4,12820]{2,0,1:T(8,128)(2,1)}), bf16[24,4,12820]{2,0,1:T(8,128)(2,1)S(1)}, u32[]{:S(2)}, u32[]{:S(2)}) async-start(bf16[24,4,12820]{2,0,1:T(8,128)(2,1)} %copy.70), calls=%async_computation.1 | async-start | bytes 4964352 | tf_op jit(solution)/shard_map/all_to_all | solution.py:81
  514.1 60.6 %all-to-all-start.2 = ((bf16[4,24,12820]{2,1,0:T(8,128)(2,1)}), bf16[4,24,12820]{2,1,0:T(8,128)(2,1)}, u32[]{:S(2)}, u32[]{:S(2)}) async-start(bf16[4,24,12820]{2,1,0:T(8,128)(2,1)} %bitcast.112), calls=%async_computation.2 | async-start | bytes 4964352 | tf_op jit(solution)/shard_map/all_to_all | solution.py:91
  645.5 6.0 copy-start.5
  645.5 6.0 copy-start.7
  645.5 6.1 copy-start.9
  645.5 6.1 copy-start.11
  645.5 178.7 %all-to-all-start.3 = ((bf16[2,24,640,2,80]{4,1,3,0,2:T(8,128)(2,1)}), bf16[2,24,640,2,80]{4,1,3,0,2:T(8,128)(2,1)}, u32[]{:S(2)}, u32[]{:S(2)}) async-start(bf16[2,24,640,2,80]{4,1,3,0,2:T(8,128)(2,1)} %copy.76), calls=%async_computation.3 | async-start | bytes 31457280 | tf_op jit(solution)/shard_map/all_to_all | solution.py:108
  824.2 33.7 %copy-start.3 = (s32[1024]{0:T(1024)S(1)}, s32[1024]{0:T(1024)}, u32[]{:S(2)}) copy-start(s32[1024]{0:T(1024)} %get-tuple-element.18) | copy-start | bytes 12292
  945.7 18.3 %copy-start.1 = (bf16[96,96]{1,0:T(8,128)(2,1)S(1)}, bf16[96,96]{1,0:T(8,128)(2,1)}, u32[]{:S(2)}) copy-start(bf16[96,96]{1,0:T(8,128)(2,1)} %param.12) | copy-start | bytes 55300
